TPU v7x, 128 devices: a whole 4x4x4 slice. The times are simulated.
128 devices in a mesh: pix: 16 (over x, y), tm: 8 (over z, core).
Axes of the slice: x: 4, y: 4, z: 4, core: 2. Of those that a mesh axis runs over, the one named last changes fastest.
Arguments:
- raw_frames: float32 [1024, 131072], P(('tm', 'pix')), may hold values from 1 to 64
- frame_order: int32 [1024], P(('tm', 'pix')), may hold values from 0 to 7, as said below
- owner_map: int32 [1024], replicated, may hold values from 0 to 1023, each once
- pixel_mask: int32 [131072], replicated, may hold values 0 or 1
- dark: float32 [131072], replicated, may hold values from 0 to 0.5
- flat: float32 [131072], replicated, may hold values from 0.5 to 1.5
- polarization: float32 [131072], replicated, may hold values from 0.5 to 1
- solid_angle: float32 [131072], replicated, may hold values from 0.6 to 1
Outputs:
- g2: float32 [4, 16, 131072], P(None, None, ('pix', 'tm'))
- mean_frame: float32 [131072], P(('pix', 'tm'))
Inputs may be any that keep to these rules, and one draw needn't show every extreme that they name: `frame_order`: each aligned block of 8 entries is a permutation of 0 .. 7. `owner_map`: a permutation of the block numbers.
All inputs are finite; a program needn't handle non-finite values.
Results may differ from a plain program's by a relative error of at most 0.0003.
Values sent between devices are 32-bit elements; how exact they have to be, the bound alone decides.
A program may use at most 128 MiB of HBM per device.

v0:
```python
import jax
import jax.numpy as jnp
from jax import lax
from jax.sharding import PartitionSpec as P

FRAMES = 1024
LAGS = 16
LEVELS = 4


def from_behind(block, axis, distance):
    devices = range(lax.axis_size(axis))
    route = [(i - distance, i) for i in devices if i - distance in devices]
    return lax.ppermute(block, axis, route)


def coarsen(series):
    return 0.5 * (series[0::2] + series[1::2])


def lag_products(series, following):
    seg_rows = series.shape[0]
    products = []
    for lag_no in range(1, LAGS + 1):
        inner = jnp.sum(series[: seg_rows - lag_no] * series[lag_no:], axis=0)
        outer = jnp.sum(series[seg_rows - lag_no :] * following[:lag_no], axis=0)
        products.append(inner + outer)
    return jnp.stack(products)


def body(raw_frames, frame_order, owner_map, pixel_mask, dark, flat, polarization, solid_angle):
    n_owners = lax.axis_size("pix")
    n_segments = lax.axis_size("tm")
    all_pixels = raw_frames.shape[1]
    owned = all_pixels // n_owners
    n_blocks = owner_map.shape[0]
    block_width = all_pixels // n_blocks
    read_rows = raw_frames.shape[0]
    selector = (frame_order[:, None] == jnp.arange(read_rows, dtype=jnp.int32)[None, :]).astype(
        jnp.float32
    )
    ordered = jnp.dot(
        selector, raw_frames, precision=lax.Precision.HIGHEST, preferred_element_type=jnp.float32
    )
    placed = jnp.take(ordered.reshape(read_rows, n_blocks, block_width), owner_map, axis=1).reshape(
        read_rows, all_pixels
    )
    owned_blocks = owned // block_width
    own_list = lax.dynamic_slice_in_dim(
        owner_map, lax.axis_index("pix") * owned_blocks, owned_blocks
    )
    response = flat * polarization * solid_angle
    stacked = jnp.stack((dark, response, pixel_mask.astype(jnp.float32))).reshape(
        3, n_blocks, block_width
    )
    own_consts = jnp.take(stacked, own_list, axis=1).reshape(3, owned)
    dark_own = own_consts[0]
    resp_own = own_consts[1]
    share_len = owned // n_segments
    slot_start = lax.axis_index("tm") * share_len
    counts = jnp.array(
        [
            [(FRAMES >> level_no) - lag_no for lag_no in range(1, LAGS + 1)]
            for level_no in range(LEVELS)
        ],
        dtype=jnp.float32,
    )[:, :, None]
    keeper = lax.dynamic_slice_in_dim(own_consts[2], slot_start, share_len, 0)
    segment = lax.all_to_all(placed, "pix", split_axis=1, concat_axis=0, tiled=True)
    corrected = (segment - dark_own) / resp_own
    totals = jnp.sum(corrected, axis=0)
    level_list = []
    series = corrected
    for level_no in range(LEVELS):
        following = from_behind(series[:LAGS], "tm", -1)
        level_list.append(lag_products(series, following))
        if level_no + 1 < LEVELS:
            series = coarsen(series)
    product = jnp.stack(level_list)
    product_all, totals_all = lax.psum((product, totals), "tm")
    product_mine = lax.dynamic_slice_in_dim(product_all, slot_start, share_len, 2)
    totals_mine = lax.dynamic_slice_in_dim(totals_all, slot_start, share_len, 0)
    mean_raw = totals_mine / FRAMES
    g2 = product_mine / (counts * mean_raw * mean_raw) * keeper
    return (g2, mean_raw * keeper)


def solution(mesh):
    return jax.shard_map(
        body,
        mesh=mesh,
        in_specs=(P(("tm", "pix"), None), P(("tm", "pix")), P(), P(), P(), P(), P(), P()),
        out_specs=(P(None, None, ("pix", "tm")), P(("pix", "tm"))),
        check_vma=False,
    )
```

profile of v0, /device:TPU:1, one launch (start us, length us, event | category | flops | bytes accessed | tf_op | source)
XLA Modules:
  0.0 347.0 jit_solution(2948552609236571027)
XLA Ops:
  8.9 6.2 %convolution_bitcast_fusion = f32[8,1024,128]{2,0,1:T(8,128)} fusion(f32[8,131072]{1,0:T(8,128)} %param.9, s32[8]{0:T(128)} %param.10), kind=kOutput, calls=%fused_computation.39 | convolution fusion | flops 100663360 | bytes 8388640 | tf_op jit(solution)/shard_map/dot_general | solution.py:42
  15.1 10.3 %gather_fusion = f32[1024,8,128]{2,1,0:T(8,128)} fusion(f32[8,1024,128]{2,0,1:T(8,128)} %convolution_bitcast_fusion, s32[1024]{0:T(1024)S(1)} %fusion.127), kind=kCustom, calls=%fused_computation | custom fusion | bytes 8392704 | tf_op jit(solution)/shard_map/jit(_take)/gather | solution.py:45
  25.5 4.8 %broadcast_select_fusion = f32[8,16,8192]{2,0,1:T(8,128)} fusion(f32[8,16,8192]{2,0,1:T(8,128)} %bitcast.97, pred[16,8192]{1,0:T(8,128)(4,1)S(1)} %bitcast.104), kind=kLoop, calls=%fused_computation.57 | loop fusion | flops 1048576 | bytes 8519680 | tf_op jit(solution)/shard_map/jit(_take)/select_n | solution.py:45
  30.3 7.8 %all-to-all-start = ((f32[8,16,8192]{2,0,1:T(8,128)}), f32[8,16,8192]{2,0,1:T(8,128)}, u32[]{:S(2)}, u32[]{:S(2)}) async-start(f32[8,16,8192]{2,0,1:T(8,128)} %broadcast_select_fusion), calls=%async_computation | async-start | bytes 8388608 | tf_op jit(solution)/shard_map/all_to_all | solution.py:69
  39.6 2.5 pad_maximum_fusion
  43.5 54.8 %all-to-all-done = f32[8,16,8192]{2,0,1:T(8,128)} async-done(((f32[8,16,8192]{2,0,1:T(8,128)}), f32[8,16,8192]{2,0,1:T(8,128)}, u32[]{:S(2)}, u32[]{:S(2)}) %all-to-all-start) | async-done | bytes 4194336 | tf_op jit(solution)/shard_map/all_to_all | solution.py:69
  98.4 2.7 fusion.7
  101.0 1.6 fusion.14
  102.7 1.2 fusion.15
  103.9 1.2 fusion.12
  105.0 1.2 fusion.16
  106.2 1.2 fusion.11
  107.4 0.9 fusion.17
  108.4 1.2 fusion.1
  109.6 1.2 fusion.2
  110.8 1.2 fusion.3
  112.0 0.9 fusion.18
  112.9 1.2 fusion.4
  114.1 1.2 fusion.13
  115.3 1.2 fusion.5
  116.5 1.2 fusion.6
  117.7 1.2 fusion.10
  118.9 0.9 slice.1005
  119.7 13.9 %slice.819 = f32[64,8192]{1,0:T(8,128)} slice(f32[128,8192]{1,0:T(8,128)} %copy-done), slice={[1:128:2], [0:8192:1]} | slice | bytes 4194304 | tf_op jit(solution)/shard_map/slice | solution.py:18
  133.6 13.7 %slice.818 = f32[64,8192]{1,0:T(8,128)} slice(f32[128,8192]{1,0:T(8,128)} %copy-done), slice={[0:128:2], [0:8192:1]} | slice | bytes 4194304 | tf_op jit(solution)/shard_map/slice | solution.py:18
  147.3 2.4 add_multiply_fusion
  149.8 0.9 fusion.30
  150.7 0.9 fusion.31
  151.6 0.9 fusion.28
  152.5 0.9 fusion.32
  153.4 0.9 fusion.27
  154.3 0.8 fusion.33
  155.1 0.9 fusion.19
  156.0 0.9 fusion.20
  158.7 0.9 fusion.29
  160.0 0.9 fusion.25
  160.9 0.9 fusion.26
  161.8 0.9 slice.1069
  162.7 4.9 %slice.885 = f32[32,8192]{1,0:T(8,128)} slice(f32[64,8192]{1,0:T(8,128)S(1)} %add_multiply_fusion), slice={[1:64:2], [0:8192:1]} | slice | bytes 2097152 | tf_op jit(solution)/shard_map/slice | solution.py:18
  167.5 4.9 %slice.884 = f32[32,8192]{1,0:T(8,128)} slice(f32[64,8192]{1,0:T(8,128)S(1)} %add_multiply_fusion), slice={[0:64:2], [0:8192:1]} | slice | bytes 2097152 | tf_op jit(solution)/shard_map/slice | solution.py:18
  172.4 1.6 add_multiply_fusion.1
  174.1 0.8 fusion.46
  181.4 0.8 fusion.41
  182.2 2.6 slice.949
  184.8 2.6 slice.948
  187.4 4.4 %collective-permute-start = (f32[16,8192]{1,0:T(8,128)}, f32[16,8192]{1,0:T(8,128)S(1)}, u32[]{:S(2)}, u32[]{:S(2)}) collective-permute-start(f32[16,8192]{1,0:T(8,128)} %slice.1005), channel_id=1, source_target_pairs={{1,0},{2,1},{3,2},{4,3},{5,4},{6,5},{7,6},{9,8},{10,9},{11,10},{12... | collective-permute-start | bytes 1572872 | tf_op jit(solution)/shard_map/ppermute | solution.py:14
  191.8 1.9 collective-permute-start.1
  193.8 1.9 collective-permute-start.2
  195.7 1.3 add_multiply_fusion.2
  197.0 2.4 collective-permute-start.3
  199.4 4.2 %fusion = f32[8192]{0:T(1024)S(1)} fusion(f32[128,8192]{1,0:T(8,128)} %copy-done), kind=kLoop, calls=%fused_computation.3 | loop fusion | flops 1974272 | bytes 7962624 | tf_op jit(solution)/shard_map/reduce_sum | solution.py:25
  248.7 3.0 stack.32
  251.8 1.7 fusion.125
  253.4 2.8 stack.34
  256.3 1.6 fusion.124
  257.9 2.5 stack.36
  260.4 1.9 multiply_reduce_fusion
  263.3 2.3 stack.39
  265.7 1.5 pad_maximum_fusion.1
  267.2 2.7 fusion.9
  269.9 24.6 %psum.15 = f32[8192]{0:T(1024)S(1)} all-reduce(f32[8192]{0:T(1024)S(1)} %fusion.9), channel_id=1, replica_groups=mesh['pix'=16,'tm'=8] {'tm'}, use_global_device_ids=true, to_apply=%region_124.125 | all-reduce | flops 8192 | bytes 65536 | tf_op jit(solution)/shard_map/psum | solution.py:80
  294.5 1.3 fusion.129
  295.8 42.4 %all-reduce.2.cloned.1.call-done = f32[4,16,8192]{2,1,0:T(8,128)} async-done(((f32[4,16,8192]{2,1,0:T(8,128)}), f32[4,16,8192]{2,1,0:T(8,128)}) %all-reduce.2.cloned.1.call-update) | async-done | bytes 2097168 | tf_op jit(solution)/shard_map/psum | solution.py:80
  338.1 1.8 divide_multiply_fusion
  (292 shorter events, 58.7 us)
Async XLA Ops:
  30.2 9.1 %copy-start.9 = (s32[131072]{0:T(1024)S(1)}, s32[131072]{0:T(1024)}, u32[]{:S(2)}) copy-start(s32[131072]{0:T(1024)} %param.12) | copy-start | bytes 1572868
  30.3 9.2 %copy-start.10 = (f32[131072]{0:T(1024)S(1)}, f32[131072]{0:T(1024)}, u32[]{:S(2)}) copy-start(f32[131072]{0:T(1024)} %param.16) | copy-start | bytes 1572868
  30.3 9.2 %copy-start.11 = (f32[131072]{0:T(1024)S(1)}, f32[131072]{0:T(1024)}, u32[]{:S(2)}) copy-start(f32[131072]{0:T(1024)} %param.14) | copy-start | bytes 1572868
  30.3 9.2 %copy-start.12 = (f32[131072]{0:T(1024)S(1)}, f32[131072]{0:T(1024)}, u32[]{:S(2)}) copy-start(f32[131072]{0:T(1024)} %param.15) | copy-start | bytes 1572868
  30.3 68.1 %all-to-all-start = ((f32[8,16,8192]{2,0,1:T(8,128)}), f32[8,16,8192]{2,0,1:T(8,128)}, u32[]{:S(2)}, u32[]{:S(2)}) async-start(f32[8,16,8192]{2,0,1:T(8,128)} %broadcast_select_fusion), calls=%async_computation | async-start | bytes 8388608 | tf_op jit(solution)/shard_map/all_to_all | solution.py:69
  38.0 300.1 %all-reduce.2.cloned.1.call-start = ((), (), s32[]{:S(2)}) async-start(), calls=%async_computation.1 | async-start | bytes 4194304 | tf_op jit(solution)/shard_map/psum | solution.py:80
  101.0 17.9 %copy-start = (f32[128,8192]{1,0:T(8,128)}, f32[128,8192]{1,0:T(8,128)S(1)}, u32[]{:S(2)}) copy-start(f32[128,8192]{1,0:T(8,128)S(1)} %fusion.7) | copy-start | bytes 12582916
  187.4 16.2 %collective-permute-start = (f32[16,8192]{1,0:T(8,128)}, f32[16,8192]{1,0:T(8,128)S(1)}, u32[]{:S(2)}, u32[]{:S(2)}) collective-permute-start(f32[16,8192]{1,0:T(8,128)} %slice.1005), channel_id=1, source_target_pairs={{1,0},{2,1},{3,2},{4,3},{5,4},{6,5},{7,6},{9,8},{10,9},{11,10},{12... | collective-permute-start | bytes 1572872 | tf_op jit(solution)/shard_map/ppermute | solution.py:14
  191.8 22.9 %collective-permute-start.1 = (f32[16,8192]{1,0:T(8,128)}, f32[16,8192]{1,0:T(8,128)S(1)}, u32[]{:S(2)}, u32[]{:S(2)}) collective-permute-start(f32[16,8192]{1,0:T(8,128)} %slice.1069), channel_id=1, source_target_pairs={{1,0},{2,1},{3,2},{4,3},{5,4},{6,5},{7,6},{9,8},{10,9},{11,10},{12... | collective-permute-start | bytes 1572872 | tf_op jit(solution)/shard_map/ppermute | solution.py:14
  193.8 32.2 %collective-permute-start.2 = (f32[16,8192]{1,0:T(8,128)S(1)}, f32[16,8192]{1,0:T(8,128)S(1)}, u32[]{:S(2)}, u32[]{:S(2)}) collective-permute-start(f32[16,8192]{1,0:T(8,128)S(1)} %slice.1133), channel_id=1, source_target_pairs={{1,0},{2,1},{3,2},{4,3},{5,4},{6,5},{7,6},{9,8},{10,9},{11,10},{12... | collective-permute-start | bytes 1572872 | tf_op jit(solution)/shard_map/ppermute | solution.py:14
  196.9 49.6 %copy-start.2 = (f32[16,8192]{1,0:T(8,128)}, f32[16,8192]{1,0:T(8,128)S(1)}, u32[]{:S(2)}) copy-start(f32[16,8192]{1,0:T(8,128)S(1)} %add_multiply_fusion.2) | copy-start | bytes 1572868
  197.0 6.7 %copy-start.1 = (f32[128,8192]{1,0:T(8,128)S(1)}, f32[128,8192]{1,0:T(8,128)}, u32[]{:S(2)}) copy-start(f32[128,8192]{1,0:T(8,128)} %copy-done) | copy-start | bytes 12582916
  197.0 6.8 %copy-start.36 = (f32[8192]{0:T(1024)S(1)}, f32[8192]{0:T(1024)}, u32[]{:S(2)}) copy-start(f32[8192]{0:T(1024)} %fusion.18) | copy-start | bytes 98308
  197.0 7.5 %copy-start.37 = (f32[8192]{0:T(1024)S(1)}, f32[8192]{0:T(1024)}, u32[]{:S(2)}) copy-start(f32[8192]{0:T(1024)} %fusion.10) | copy-start | bytes 98308
  197.0 8.3 %copy-start.35 = (f32[8192]{0:T(1024)S(1)}, f32[8192]{0:T(1024)}, u32[]{:S(2)}) copy-start(f32[8192]{0:T(1024)} %fusion.11) | copy-start | bytes 98308
  197.0 40.3 %collective-permute-start.3 = (f32[16,8192]{1,0:T(8,128)S(1)}, f32[16,8192]{1,0:T(8,128)S(1)}, u32[]{:S(2)}, u32[]{:S(2)}) collective-permute-start(f32[16,8192]{1,0:T(8,128)S(1)} %add_multiply_fusion.2), channel_id=1, source_target_pairs={{1,0},{2,1},{3,2},{4,3},{5,4},{6,5},{7,6},{9,8},{10,9},{11,10},{12... | collective-permute-start | bytes 1572872 | tf_op jit(solution)/shard_map/ppermute | solution.py:14
  205.1 4.7 %copy-start.29 = (f32[8192]{0:T(1024)S(1)}, f32[8192]{0:T(1024)}, u32[]{:S(2)}) copy-start(f32[8192]{0:T(1024)} %fusion.17) | copy-start | bytes 98308
  205.9 5.4 %copy-start.26 = (f32[8192]{0:T(1024)S(1)}, f32[8192]{0:T(1024)}, u32[]{:S(2)}) copy-start(f32[8192]{0:T(1024)} %fusion.1) | copy-start | bytes 98308
  206.0 5.9 %copy-start.25 = (f32[8192]{0:T(1024)S(1)}, f32[8192]{0:T(1024)}, u32[]{:S(2)}) copy-start(f32[8192]{0:T(1024)} %fusion.2) | copy-start | bytes 98308
  206.7 6.0 %copy-start.23 = (f32[8192]{0:T(1024)S(1)}, f32[8192]{0:T(1024)}, u32[]{:S(2)}) copy-start(f32[8192]{0:T(1024)} %fusion.3) | copy-start | bytes 98308
  206.8 6.6 %copy-start.24 = (f32[8192]{0:T(1024)S(1)}, f32[8192]{0:T(1024)}, u32[]{:S(2)}) copy-start(f32[8192]{0:T(1024)} %fusion.5) | copy-start | bytes 98308
  206.8 7.3 %copy-start.22 = (f32[8192]{0:T(1024)S(1)}, f32[8192]{0:T(1024)}, u32[]{:S(2)}) copy-start(f32[8192]{0:T(1024)} %fusion.4) | copy-start | bytes 98308
  207.6 7.3 %copy-start.27 = (f32[8192]{0:T(1024)S(1)}, f32[8192]{0:T(1024)}, u32[]{:S(2)}) copy-start(f32[8192]{0:T(1024)} %fusion.34) | copy-start | bytes 98308
  208.4 7.3 %copy-start.28 = (f32[8192]{0:T(1024)S(1)}, f32[8192]{0:T(1024)}, u32[]{:S(2)}) copy-start(f32[8192]{0:T(1024)} %fusion.26) | copy-start | bytes 98308
  209.1 7.3 %copy-start.20 = (f32[8192]{0:T(1024)S(1)}, f32[8192]{0:T(1024)}, u32[]{:S(2)}) copy-start(f32[8192]{0:T(1024)} %fusion.27) | copy-start | bytes 98308
  210.5 6.7 %copy-start.19 = (f32[8192]{0:T(1024)S(1)}, f32[8192]{0:T(1024)}, u32[]{:S(2)}) copy-start(f32[8192]{0:T(1024)} %fusion.28) | copy-start | bytes 98308
  211.9 6.1 %copy-start.21 = (f32[8192]{0:T(1024)S(1)}, f32[8192]{0:T(1024)}, u32[]{:S(2)}) copy-start(f32[8192]{0:T(1024)} %fusion.29) | copy-start | bytes 98308
  214.8 10.5 %copy-start.7 = (f32[16,8192]{1,0:T(8,128)}, f32[16,8192]{1,0:T(8,128)S(1)}, u32[]{:S(2)}) copy-start(f32[16,8192]{1,0:T(8,128)S(1)} %collective-permute-done.1) | copy-start | bytes 1572868
  216.3 4.7 %copy-start.15 = (f32[8192]{0:T(1024)S(1)}, f32[8192]{0:T(1024)}, u32[]{:S(2)}) copy-start(f32[8192]{0:T(1024)} %fusion.33) | copy-start | bytes 98308
  216.4 5.3 %copy-start.14 = (f32[8192]{0:T(1024)S(1)}, f32[8192]{0:T(1024)}, u32[]{:S(2)}) copy-start(f32[8192]{0:T(1024)} %fusion.19) | copy-start | bytes 98308
  217.1 5.4 %copy-start.13 = (f32[8192]{0:T(1024)S(1)}, f32[8192]{0:T(1024)}, u32[]{:S(2)}) copy-start(f32[8192]{0:T(1024)} %fusion.20) | copy-start | bytes 98308
  218.7 7.4 %copy-start.57 = (f32[8192]{0:T(1024)S(1)}, f32[8192]{0:T(1024)}, u32[]{:S(2)}) copy-start(f32[8192]{0:T(1024)} %fusion.42) | copy-start | bytes 98308
  219.5 7.4 %copy-start.56 = (f32[8192]{0:T(1024)S(1)}, f32[8192]{0:T(1024)}, u32[]{:S(2)}) copy-start(f32[8192]{0:T(1024)} %fusion.43) | copy-start | bytes 98308
  220.3 7.4 %copy-start.54 = (f32[8192]{0:T(1024)S(1)}, f32[8192]{0:T(1024)}, u32[]{:S(2)}) copy-start(f32[8192]{0:T(1024)} %fusion.44) | copy-start | bytes 98308
  221.7 6.7 %copy-start.53 = (f32[8192]{0:T(1024)S(1)}, f32[8192]{0:T(1024)}, u32[]{:S(2)}) copy-start(f32[8192]{0:T(1024)} %fusion.45) | copy-start | bytes 98308
  223.1 6.1 %copy-start.52 = (f32[8192]{0:T(1024)S(1)}, f32[8192]{0:T(1024)}, u32[]{:S(2)}) copy-start(f32[8192]{0:T(1024)} %fusion.46) | copy-start | bytes 98308
  225.3 4.7 %copy-start.51 = (f32[8192]{0:T(1024)S(1)}, f32[8192]{0:T(1024)}, u32[]{:S(2)}) copy-start(f32[8192]{0:T(1024)} %fusion.47) | copy-start | bytes 98308
  226.0 10.4 %copy-start.6 = (f32[16,8192]{1,0:T(8,128)}, f32[16,8192]{1,0:T(8,128)S(1)}, u32[]{:S(2)}) copy-start(f32[16,8192]{1,0:T(8,128)S(1)} %collective-permute-done.2) | copy-start | bytes 1572868
  237.3 9.3 %copy-start.4 = (f32[16,8192]{1,0:T(8,128)}, f32[16,8192]{1,0:T(8,128)S(1)}, u32[]{:S(2)}) copy-start(f32[16,8192]{1,0:T(8,128)S(1)} %collective-permute-done.3) | copy-start | bytes 1572868
  241.6 6.4 %copy-start.38 = (f32[8192]{0:T(1024)S(1)}, f32[8192]{0:T(1024)}, u32[]{:S(2)}) copy-start(f32[8192]{0:T(1024)} %fusion.6) | copy-start | bytes 98308
  241.8 6.9 %copy-start.41 = (f32[8192]{0:T(1024)S(1)}, f32[8192]{0:T(1024)}, u32[]{:S(2)}) copy-start(f32[8192]{0:T(1024)} %add.845) | copy-start | bytes 98308
  241.8 6.9 %copy-start.42 = (f32[8192]{0:T(1024)S(1)}, f32[8192]{0:T(1024)}, u32[]{:S(2)}) copy-start(f32[8192]{0:T(1024)} %add.843) | copy-start | bytes 98308
  241.8 6.9 %copy-start.43 = (f32[8192]{0:T(1024)S(1)}, f32[8192]{0:T(1024)}, u32[]{:S(2)}) copy-start(f32[8192]{0:T(1024)} %add.841) | copy-start | bytes 98308
  241.8 6.9 %copy-start.44 = (f32[8192]{0:T(1024)S(1)}, f32[8192]{0:T(1024)}, u32[]{:S(2)}) copy-start(f32[8192]{0:T(1024)} %add.839) | copy-start | bytes 98308
  241.8 6.9 %copy-start.45 = (f32[8192]{0:T(1024)S(1)}, f32[8192]{0:T(1024)}, u32[]{:S(2)}) copy-start(f32[8192]{0:T(1024)} %add.837) | copy-start | bytes 98308
  241.8 6.9 %copy-start.46 = (f32[8192]{0:T(1024)S(1)}, f32[8192]{0:T(1024)}, u32[]{:S(2)}) copy-start(f32[8192]{0:T(1024)} %add.835) | copy-start | bytes 98308
  241.8 6.9 %copy-start.47 = (f32[8192]{0:T(1024)S(1)}, f32[8192]{0:T(1024)}, u32[]{:S(2)}) copy-start(f32[8192]{0:T(1024)} %add.833) | copy-start | bytes 98308
  241.8 6.9 %copy-start.48 = (f32[8192]{0:T(1024)S(1)}, f32[8192]{0:T(1024)}, u32[]{:S(2)}) copy-start(f32[8192]{0:T(1024)} %add.831) | copy-start | bytes 98308
  243.1 8.7 %copy-start.39 = (f32[8192]{0:T(1024)S(1)}, f32[8192]{0:T(1024)}, u32[]{:S(2)}) copy-start(f32[8192]{0:T(1024)} %fusion.25) | copy-start | bytes 98308
  243.3 13.0 %copy-start.40 = (f32[8192]{0:T(1024)S(1)}, f32[8192]{0:T(1024)}, u32[]{:S(2)}) copy-start(f32[8192]{0:T(1024)} %fusion.41) | copy-start | bytes 98308
  251.7 11.6 %copy-start.55 = (f32[8192]{0:T(1024)S(1)}, f32[8192]{0:T(1024)}, u32[]{:S(2)}) copy-start(f32[8192]{0:T(1024)} %add.925) | copy-start | bytes 98308
  251.7 11.6 %copy-start.58 = (f32[8192]{0:T(1024)S(1)}, f32[8192]{0:T(1024)}, u32[]{:S(2)}) copy-start(f32[8192]{0:T(1024)} %add.927) | copy-start | bytes 98308
  251.7 11.6 %copy-start.59 = (f32[8192]{0:T(1024)S(1)}, f32[8192]{0:T(1024)}, u32[]{:S(2)}) copy-start(f32[8192]{0:T(1024)} %add.923) | copy-start | bytes 98308
  251.7 11.6 %copy-start.60 = (f32[8192]{0:T(1024)S(1)}, f32[8192]{0:T(1024)}, u32[]{:S(2)}) copy-start(f32[8192]{0:T(1024)} %add.929) | copy-start | bytes 98308
  251.7 11.6 %copy-start.61 = (f32[8192]{0:T(1024)S(1)}, f32[8192]{0:T(1024)}, u32[]{:S(2)}) copy-start(f32[8192]{0:T(1024)} %add.921) | copy-start | bytes 98308
  251.7 11.6 %copy-start.62 = (f32[8192]{0:T(1024)S(1)}, f32[8192]{0:T(1024)}, u32[]{:S(2)}) copy-start(f32[8192]{0:T(1024)} %add.931) | copy-start | bytes 98308
  251.7 11.6 %copy-start.63 = (f32[8192]{0:T(1024)S(1)}, f32[8192]{0:T(1024)}, u32[]{:S(2)}) copy-start(f32[8192]{0:T(1024)} %add.919) | copy-start | bytes 98308
  251.7 11.6 %copy-start.64 = (f32[8192]{0:T(1024)S(1)}, f32[8192]{0:T(1024)}, u32[]{:S(2)}) copy-start(f32[8192]{0:T(1024)} %add.933) | copy-start | bytes 98308
  253.4 8.9 %copy-start.3 = (f32[16,8192]{1,0:T(8,128)S(1)}, f32[16,8192]{1,0:T(8,128)}, u32[]{:S(2)}) copy-start(f32[16,8192]{1,0:T(8,128)} %copy-done.2) | copy-start | bytes 1572868
  253.4 8.9 %copy-start.5 = (f32[16,8192]{1,0:T(8,128)S(1)}, f32[16,8192]{1,0:T(8,128)}, u32[]{:S(2)}) copy-start(f32[16,8192]{1,0:T(8,128)} %copy-done.4) | copy-start | bytes 1572868
  253.4 9.9 %copy-start.65 = (f32[8192]{0:T(1024)S(1)}, f32[8192]{0:T(1024)}, u32[]{:S(2)}) copy-start(f32[8192]{0:T(1024)} %add.917) | copy-start | bytes 98308
  253.4 12.2 %copy-start.8 = (f32[16,8192]{1,0:T(8,128)S(1)}, f32[16,8192]{1,0:T(8,128)}, u32[]{:S(2)}) copy-start(f32[16,8192]{1,0:T(8,128)} %stack.32) | copy-start | bytes 1572868
  257.9 5.4 %copy-start.66 = (f32[8192]{0:T(1024)S(1)}, f32[8192]{0:T(1024)}, u32[]{:S(2)}) copy-start(f32[8192]{0:T(1024)} %add.937) | copy-start | bytes 98308
  267.2 71.0 %copy-start.67 = (f32[4,16]{1,0:T(4,128)S(1)}, f32[4,16]{1,0:T(4,128)}, u32[]{:S(2)}) copy-start(f32[4,16]{1,0:T(4,128)} %constant.54.clone) | copy-start | bytes 772
  (10 other events, 41.9 us)
Sparse Core Ops, SparseCore 0:
  267.3 70.7 all-reduce.1
where the time goes:
time: 353 us; the launch traced here: 347 us
  other arithmetic  117 us (33%)
  waiting for transfers between devices  97.2 us (28%)
  local copies, waits for them, and re-layouts  67.3 us (19%)
  blocking collectives  24.6 us (7%)
  starting transfers between devices  19 us (5%)
  between operations  15.5 us (4%)
  matrix products  6.2 us (2%)
    all_to_all x1, waiting for transfers between devices, body(): lax.all_to_all(placed, 'pix', split_axis=1, concat_axis=0, tiled=True)  54.8 us
    reduce_sum x53, other arithmetic, lag_products(): inner = jnp.sum(series[:seg_rows - lag_no] * series[lag_no:], axis=0)  43.2 us
    slice x6, local copies, waits for them, and re-layouts, coarsen(): return 0.5 * (series[0::2] + series[1::2])  42.5 us
    psum x1, waiting for transfers between devices, body(): product_all, totals_all = lax.psum((product, totals), 'tm')  42.4 us
    add x62, other arithmetic, lag_products(): products.append(inner + outer)  39.9 us
    psum x1, blocking collectives, body(): product_all, totals_all = lax.psum((product, totals), 'tm')  24.6 us
    another operation x4, local copies, waits for them, and re-layouts, lag_products(): return jnp.stack(products)  10.7 us
    ppermute x4, starting transfers between devices, from_behind(): return lax.ppermute(block, axis, route)  10.6 us
  transfers between devices with their start and end apart: 6, of which 2 were waited for; matrix products, arithmetic and copies ran while one was open for 14% of the time, Pallas kernels for 0%

commit v1 on v0

v1 whole, which is shorter than its diff:
```python
import jax
import jax.numpy as jnp
from jax import lax
from jax.experimental import pallas as pl
from jax.experimental.pallas import tpu as pltpu
from jax.sharding import PartitionSpec as P

FRAMES = 1024
LAGS = 16
LEVELS = 4
READ = 8
BLK = 128
N_PIX = 16
N_TM = 8
SIDE = 4
N_DEV = N_PIX * N_TM
SEG = FRAMES // N_TM
GROUP = 4
MESH = pl.DeviceIdType.MESH


def step_offset(phase):
    return ((phase + 1) // 2) * (2 * (phase % 2) - 1)


def step_target(step, pix, tm):
    phase, turn = step // N_PIX, step % N_PIX
    to_x = (pix // SIDE + turn % SIDE) % SIDE
    to_y = (pix % SIDE + turn // SIDE) % SIDE
    to_tm = (tm - step_offset(phase) + N_TM) % N_TM
    return to_x * SIDE + to_y, to_tm


def lag_group(fresh, before, sums):
    rows = before + fresh
    sums = list(sums)
    for i in range(LAGS):
        for lag in range(1, LAGS + 1):
            sums[lag - 1] = sums[lag - 1] + fresh[i] * rows[LAGS + i - lag]
    return sums


def stage_kernel(owner, order, raw_in, dark_in, flat_in, pol_in, solid_in, mask_in, staged, consts,
                 raw_v, tmp, stage, rows_v, mask_v, load_sem, row_sem, mask_sem, out_sem):
    pix = lax.axis_index("pix")
    tm = lax.axis_index("tm")
    me = pix * N_TM + tm

    load = pltpu.make_async_copy(raw_in, raw_v, load_sem)
    load.start()
    for j in range(8):
        block = owner[me * 8 + j]
        for i, src in enumerate((dark_in, flat_in, pol_in, solid_in)):
            pltpu.make_async_copy(src.at[pl.ds(block, 1)], rows_v.at[i, pl.ds(j, 1)], row_sem).start()
        pltpu.make_async_copy(mask_in.at[pl.ds(block, 1)], mask_v.at[pl.ds(j, 1)], mask_sem).start()
    load.wait()

    def put(turn, carry):
        step0 = turn * GROUP
        for u in range(GROUP):
            to_pix, to_tm = step_target(step0 + u, pix, tm)
            base = (to_pix * N_TM + to_tm) * 8
            for j in range(8):
                block = owner[base + j]
                tmp[u, pl.ds(j, 8, stride=8), :] = raw_v[:, pl.ds(pl.multiple_of(block * BLK, BLK), BLK)]
        for u in range(GROUP):
            for r in range(READ):
                stage[step0 + u, r] = tmp[u, pl.ds(pl.multiple_of(order[r] * 8, 8), 8), :]
        part = pl.ds(step0, GROUP)
        pltpu.make_async_copy(stage.at[part], staged.at[part], out_sem).start()
        return carry

    lax.fori_loop(0, N_DEV // GROUP, put, 0)
    pltpu.make_async_copy(rows_v, rows_v, row_sem).wait()
    pltpu.make_async_copy(mask_v, mask_v, mask_sem).wait()
    consts[0] = rows_v[0]
    consts[1] = rows_v[1] * rows_v[2] * rows_v[3]
    consts[2] = mask_v[...].astype(jnp.float32)
    pltpu.make_async_copy(stage, stage, out_sem).wait()


def kernel(staged, consts, g2_out, mean_out, tmp, xs, s1, s2, s3, sums, own_sem, send_sem, recv_sem):
    pix = lax.axis_index("pix")
    tm = lax.axis_index("tm")
    barrier = pltpu.get_barrier_semaphore()

    def greet(step, carry):
        to_pix, to_tm = step_target(step, pix, tm)
        pl.semaphore_signal(barrier, inc=1, device_id={"pix": to_pix, "tm": to_tm}, device_id_type=MESH)
        return carry

    lax.fori_loop(1, N_DEV, greet, 0)

    zero = jnp.zeros((8, BLK), jnp.float32)
    for buf in (xs, s1, s2, s3):
        for i in range(LAGS):
            buf[i] = zero
    for level in range(LEVELS):
        for lag in range(LAGS):
            sums[level, lag] = zero
    dark = consts[0]
    inverse = 1.0 / consts[1]

    my_rows = xs.at[pl.ds(LAGS + tm * SEG + pix * READ, READ)]

    def send(step, carry):
        to_pix, to_tm = step_target(step, pix, tm)
        pltpu.make_async_remote_copy(
            src_ref=staged.at[step],
            dst_ref=my_rows,
            send_sem=send_sem,
            recv_sem=recv_sem.at[tm],
            device_id={"pix": to_pix, "tm": to_tm},
            device_id_type=MESH,
        ).start()
        return carry

    own = pltpu.make_async_copy(staged.at[0], my_rows, own_sem)
    own.start()
    pl.semaphore_wait(barrier, N_DEV - 1)
    lax.fori_loop(1, N_DEV, send, 0)
    own.wait()

    def level_pass(level, buf, deeper, seg, joined):
        rows = SEG >> level
        first = LAGS + seg * rows

        def group(g, acc):
            start = first + g * LAGS
            fresh = [buf[start + i] for i in range(LAGS)]
            if level == 0:
                fresh = [(one - dark) * inverse for one in fresh]
                for i in range(LAGS):
                    buf[start + i] = fresh[i]
            back = jnp.where((g > 0) | joined, start - LAGS, 0)
            before = [buf[back + i] for i in range(LAGS)]
            if deeper is not None:
                for i in range(LAGS // 2):
                    deeper[LAGS + (seg * rows + g * LAGS) // 2 + i] = 0.5 * (fresh[2 * i] + fresh[2 * i + 1])
            return tuple(lag_group(fresh, before, acc))

        acc = tuple(sums[level, lag] for lag in range(LAGS))
        acc = lax.fori_loop(0, rows // LAGS, group, acc)
        for lag in range(LAGS):
            sums[level, lag] = acc[lag]

    def border(seg):
        for level, buf in enumerate((xs, s1, s2, s3)):
            first = LAGS + seg * (SEG >> level)
            rows = [buf[first - LAGS + i] for i in range(2 * LAGS)]
            for lag in range(1, LAGS + 1):
                part = sums[level, lag - 1]
                for i in range(lag):
                    part = part + rows[LAGS + i] * rows[LAGS + i - lag]
                sums[level, lag - 1] = part

    def segment(phase, carry):
        offset = step_offset(phase)
        seg = (tm + offset + N_TM) % N_TM

        @pl.when(phase == 0)
        def _():
            part = xs.at[pl.ds(LAGS, (N_PIX - 1) * READ)]
            pltpu.make_async_copy(part, part, recv_sem.at[seg]).wait()

        @pl.when(phase > 0)
        def _():
            part = xs.at[pl.ds(LAGS, N_PIX * READ)]
            pltpu.make_async_copy(part, part, recv_sem.at[seg]).wait()

        joined = (offset > 0) & (seg > 0)
        for level, (buf, deeper) in enumerate(((xs, s1), (s1, s2), (s2, s3), (s3, None))):
            level_pass(level, buf, deeper, seg, joined)
        after = (seg + 1) % N_TM

        @pl.when(((offset < 0) | (phase == N_TM - 1)) & (after > 0))
        def _():
            border(after)

        return carry

    lax.fori_loop(0, N_TM, segment, 0)

    total = s3[LAGS]
    for i in range(1, FRAMES >> 3):
        total = total + s3[LAGS + i]
    mean = total / (FRAMES >> 3)
    keeper = consts[2]
    scale = keeper / (mean * mean)
    shown = mean * keeper
    mean_out[...] = shown
    flat_sums = tmp
    for level in range(LEVELS):
        for half in range(2):
            for k in range(8):
                lag = half * 8 + k
                flat_sums[half, pl.ds(k * 8, 8), :] = sums[level, lag] * (scale * (1.0 / ((FRAMES >> level) - lag - 1)))
            for j in range(8):
                g2_out[level, pl.ds(half * 8, 8), pl.ds(j * BLK, BLK)] = flat_sums[half, pl.ds(j, 8, stride=8), :]

    sent = xs.at[pl.ds(LAGS, (N_DEV - 1) * READ)]
    pltpu.make_async_copy(sent, sent, send_sem).wait()


def body(raw_frames, frame_order, owner_map, pixel_mask, dark, flat, polarization, solid_angle):
    n_blocks = owner_map.shape[0]
    tiles = [a.reshape(n_blocks, BLK) for a in (dark, flat, polarization, solid_angle, pixel_mask)]
    hbm = pl.BlockSpec(memory_space=pl.ANY)
    smem = pl.BlockSpec(memory_space=pltpu.SMEM)
    vmem = pl.BlockSpec(memory_space=pltpu.VMEM)
    f32 = jnp.float32
    staged, consts = pl.pallas_call(
        stage_kernel,
        out_shape=(
            jax.ShapeDtypeStruct((N_DEV, READ, 8, BLK), f32),
            jax.ShapeDtypeStruct((3, 8, BLK), f32),
        ),
        in_specs=[smem, smem] + [hbm] * 6,
        out_specs=(hbm, vmem),
        scratch_shapes=[
            pltpu.VMEM(raw_frames.shape, f32),
            pltpu.VMEM((GROUP, 64, BLK), f32),
            pltpu.VMEM((N_DEV, READ, 8, BLK), f32),
            pltpu.VMEM((4, 8, BLK), f32),
            pltpu.VMEM((8, BLK), jnp.int32),
            pltpu.SemaphoreType.DMA,
            pltpu.SemaphoreType.DMA,
            pltpu.SemaphoreType.DMA,
            pltpu.SemaphoreType.DMA,
        ],
    )(owner_map, frame_order, raw_frames, *tiles)
    g2, mean = pl.pallas_call(
        kernel,
        out_shape=(
            jax.ShapeDtypeStruct((LEVELS, LAGS, 8 * BLK), f32),
            jax.ShapeDtypeStruct((8, BLK), f32),
        ),
        in_specs=[hbm, vmem],
        out_specs=(vmem, vmem),
        scratch_shapes=[
            pltpu.VMEM((2, 64, BLK), f32),
            pltpu.VMEM((LAGS + FRAMES, 8, BLK), f32),
            pltpu.VMEM((LAGS + FRAMES // 2, 8, BLK), f32),
            pltpu.VMEM((LAGS + FRAMES // 4, 8, BLK), f32),
            pltpu.VMEM((LAGS + FRAMES // 8, 8, BLK), f32),
            pltpu.VMEM((LEVELS, LAGS, 8, BLK), f32),
            pltpu.SemaphoreType.DMA,
            pltpu.SemaphoreType.DMA,
            pltpu.SemaphoreType.DMA((N_TM,)),
        ],
        compiler_params=pltpu.CompilerParams(collective_id=0, has_side_effects=True),
    )(staged, consts)
    return g2, mean.reshape(8 * BLK)


def solution(mesh):
    return jax.shard_map(
        body,
        mesh=mesh,
        in_specs=(P(("tm", "pix"), None), P(("tm", "pix")), P(), P(), P(), P(), P(), P()),
        out_specs=(P(None, None, ("pix", "tm")), P(("pix", "tm"))),
        check_vma=False,
    )
```

time: 353 us -> 94.7 us (0.27); the launches traced: 347 us -> 94.4 us
  other arithmetic: 117 us -> 0 us
  waiting for transfers between devices: 97.2 us -> 0 us
  Pallas kernels: 0 us -> 90.8 us
  local copies, waits for them, and re-layouts: 67.3 us -> 2.94 us
  blocking collectives: 24.6 us -> 0 us
  starting transfers between devices: 19 us -> 0 us
  between operations: 15.5 us -> 0.65 us
  matrix products: 6.2 us -> 0 us
    pallas_call x0 -> x2, Pallas kernels: none -> 90.8 us  [the longest x1 79.8 us: body(): pl.pallas_call(kernel, out_shape=(jax.ShapeDtypeStruct((LEVELS, LAGS, 8 *...]
    reduce_sum x108 -> x0, other arithmetic: 55.1 us -> none  [the longest x53 43.2 us: lag_products(): inner = jnp.sum(series[:seg_rows - lag_no] * series[lag_no:], axis=0)]
    all_to_all x1 -> x0, waiting for transfers between devices: 54.8 us -> none  [body(): lax.all_to_all(placed, 'pix', split_axis=1, concat_axis=0, tiled=True)]
    slice x10 -> x0, local copies, waits for them, and re-layouts: 45 us -> none  [the longest x6 42.5 us: coarsen(): return 0.5 * (series[0::2] + series[1::2])]
    psum x1 -> x0, waiting for transfers between devices: 42.4 us -> none  [body(): product_all, totals_all = lax.psum((product, totals), 'tm')]
    add x62 -> x0, other arithmetic: 39.9 us -> none  [lag_products(): products.append(inner + outer)]
    psum x1 -> x0, blocking collectives: 24.6 us -> none  [body(): product_all, totals_all = lax.psum((product, totals), 'tm')]
    gather x2 -> x0, local copies, waits for them, and re-layouts: 11 us -> none  [the longest x1 10.3 us: body(): jnp.take(ordered.reshape(read_rows, n_blocks, block_width), owner_map, ax...]
  transfers between devices with their start and end apart: 6 -> 0, of which waited for: 2 -> 0; matrix products, arithmetic and copies ran while one was open for 14% -> 0% of each run, Pallas kernels for 0% -> 0%
where the time goes in v1:
time: 94.7 us; the launch traced here: 94.4 us
  Pallas kernels  90.8 us (96%)
  local copies, waits for them, and re-layouts  2.94 us (3%)
    pallas_call x1, Pallas kernels, body(): pl.pallas_call(kernel, out_shape=(jax.ShapeDtypeStruct((LEVELS, LAGS, 8 *...  79.8 us
    pallas_call x1, Pallas kernels, body(): pl.pallas_call(stage_kernel, out_shape=(jax.ShapeDtypeStruct((N_DEV, READ...  11 us
    unnamed x2, local copies, waits for them, and re-layouts  2.94 us

profile of v1, /device:TPU:1, one launch (start us, length us, event | category | flops | bytes accessed | tf_op | source)
XLA Modules:
  0.0 94.4 jit_solution(2270254499332977889)
XLA Ops:
  0.6 11.0 %shard_map.95 = (f32[128,8,8,128]{3,2,1,0:T(8,128)}, f32[3,8,128]{2,1,0:T(8,128)}) custom-call(s32[1024]{0:T(1024)} %owner.1, s32[8]{0:T(128)} %order.1, f32[8,131072]{1,0:T(8,128)} %raw_in.1, f32[1024,128]{1,0:T(8,128)} %bitcast.6, f32[1024,128]{1,0:T(8,128)} %bitcast.7, f32[1024,128]{1,0:T(8,128)} %bitcast.8, f32[1024,128]{1,0:T(8,128)} %bitcast.9, ...), custom_call_target="tpu_custom_call" | custom-call | tf_op jit(solution)/shard_map/pallas_call | solution.py:212
  11.6 79.8 %shard_map.96 = (f32[4,16,1024]{2,1,0:T(8,128)}, f32[8,128]{1,0:T(8,128)}) custom-call(f32[128,8,8,128]{3,2,1,0:T(8,128)} %get-tuple-element.6.staged, f32[3,8,128]{2,1,0:T(8,128)} %get-tuple-element.7.consts), custom_call_target="tpu_custom_call" | custom-call | tf_op jit(solution)/shard_map/pallas_call | solution.py:232
  91.5 1.7 %copy.12 = f32[4,16,1024]{2,1,0:T(8,128)} copy(f32[4,16,1024]{2,1,0:T(8,128)} %get-tuple-element.12) | data formatting | bytes 524288
  93.1 1.3 %copy.13 = f32[1024]{0:T(1024)} copy(f32[1024]{0:T(1024)} %bitcast.11) | data formatting | bytes 8192

commit v2 on v1

v2 whole, which is shorter than its diff:
```python
import jax
import jax.numpy as jnp
from jax import lax
from jax.experimental import pallas as pl
from jax.experimental.pallas import tpu as pltpu
from jax.sharding import PartitionSpec as P

FRAMES = 1024
LAGS = 16
LEVELS = 4
READ = 8
BLK = 128
N_PIX = 16
N_TM = 8
SIDE = 4
N_DEV = N_PIX * N_TM
SEG = FRAMES // N_TM
GROUP = 4
MESH = pl.DeviceIdType.MESH


ORDER = (0, 4, 1, -1, 3, -3, 2, -2)


def pick(table, index):
    value = table[0]
    for i, entry in enumerate(table[1:], 1):
        value = jnp.where(index == i, entry, value)
    return value


def before_done(phase, side):
    return int(any((ORDER[phase] + side - done) % N_TM == 0 for done in ORDER[:phase]))


def step_target(step, pix, tm):
    turn = lax.rem(step, 32)
    at = lax.div(turn, 2)
    offset = pick(ORDER, lax.div(step, 32) * 2 + lax.rem(turn, 2))
    x, y = lax.div(pix, SIDE), lax.rem(pix, SIDE)
    to_x = lax.rem(x + at, SIDE)
    to_y = lax.rem(y + at + lax.div(at, SIDE), SIDE)
    return to_x * SIDE + to_y, lax.rem(tm - offset + N_TM, N_TM)


def lag_group(fresh, before, sums):
    rows = before + fresh
    sums = list(sums)
    for i in range(LAGS):
        for lag in range(1, LAGS + 1):
            sums[lag - 1] = sums[lag - 1] + fresh[i] * rows[LAGS + i - lag]
    return sums


def kernel(owner, order, raw_in, dark_in, flat_in, pol_in, solid_in, mask_in, g2_out, mean_out,
           raw_v, tmp, stage, xs, s1, s2, s3, sums, consts, dark_v, flat_v, pol_v, solid_v, mask_v,
           load_sem, const_sem, own_sem, send_sem, recv_sem):
    pix = lax.axis_index("pix")
    tm = lax.axis_index("tm")
    me = pix * N_TM + tm

    load = pltpu.make_async_copy(raw_in, raw_v, load_sem)
    load.start()

    barrier = pltpu.get_barrier_semaphore()

    def greet(step, carry):
        to = lax.rem(me + step, N_DEV)
        peer = {"pix": lax.div(to, N_TM), "tm": lax.rem(to, N_TM)}
        pl.semaphore_signal(barrier, inc=1, device_id=peer, device_id_type=MESH)
        return carry

    lax.fori_loop(1, N_DEV, greet, 0)

    const_copies = [
        pltpu.make_async_copy(src, dst, const_sem.at[i])
        for i, (src, dst) in enumerate(
            ((dark_in, dark_v), (flat_in, flat_v), (pol_in, pol_v), (solid_in, solid_v), (mask_in, mask_v))
        )
    ]
    for copy in const_copies:
        copy.start()

    zero = jnp.zeros((8, BLK), jnp.float32)
    for buf in (xs, s1, s2, s3):
        for i in range(LAGS):
            buf[i] = zero
    for level in range(LEVELS):
        for lag in range(LAGS):
            sums[level, lag] = zero
    load.wait()
    rows_tmp = tmp.reshape(GROUP, 64, BLK)

    def put(turn, carry):
        for u in range(GROUP):
            to = turn * GROUP + u
            for j in range(8):
                rows_tmp[u, pl.ds(j, 8, stride=8), :] = raw_v[owner[to * 8 + j]]
        for u in range(GROUP):
            for r in range(READ):
                stage[turn * GROUP + u, r] = tmp[u, order[r]]
        return carry

    lax.fori_loop(0, N_DEV // GROUP, put, 0)

    for copy in const_copies:
        copy.wait()
    for j in range(8):
        block = owner[me * 8 + j]
        consts[0, j] = dark_v[block]
        consts[1, j] = flat_v[block] * pol_v[block] * solid_v[block]
        consts[2, j] = mask_v[block].astype(jnp.float32)
    dark = consts[0]
    inverse = 1.0 / consts[1]

    my_rows = xs.at[pl.ds(LAGS + tm * SEG + pix * READ, READ)]

    def send(step, carry):
        to_pix, to_tm = step_target(step, pix, tm)
        pltpu.make_async_remote_copy(
            src_ref=stage.at[to_pix * N_TM + to_tm],
            dst_ref=my_rows,
            send_sem=send_sem,
            recv_sem=recv_sem.at[tm],
            device_id={"pix": to_pix, "tm": to_tm},
            device_id_type=MESH,
        ).start()
        return carry

    own = pltpu.make_async_copy(stage.at[me], my_rows, own_sem)
    own.start()
    pl.semaphore_wait(barrier, N_DEV - 1)
    lax.fori_loop(1, N_DEV, send, 0)
    own.wait()

    def level_pass(level, buf, deeper, seg, joined):
        rows = SEG >> level
        first = LAGS + seg * rows

        def group(g, acc):
            start = first + g * LAGS
            fresh = [buf[start + i] for i in range(LAGS)]
            if level == 0:
                fresh = [(one - dark) * inverse for one in fresh]
                for i in range(LAGS):
                    buf[start + i] = fresh[i]
            back = jnp.where((g > 0) | joined, start - LAGS, 0)
            before = [buf[back + i] for i in range(LAGS)]
            if deeper is not None:
                for i in range(LAGS // 2):
                    deeper[LAGS + (seg * rows + g * LAGS) // 2 + i] = 0.5 * (fresh[2 * i] + fresh[2 * i + 1])
            return tuple(lag_group(fresh, before, acc))

        acc = tuple(sums[level, lag] for lag in range(LAGS))
        acc = lax.fori_loop(0, rows // LAGS, group, acc)
        for lag in range(LAGS):
            sums[level, lag] = acc[lag]

    def border(seg):
        for level, buf in enumerate((xs, s1, s2, s3)):
            first = LAGS + seg * (SEG >> level)
            rows = [buf[first - LAGS + i] for i in range(2 * LAGS)]
            for lag in range(1, LAGS + 1):
                part = sums[level, lag - 1]
                for i in range(lag):
                    part = part + rows[LAGS + i] * rows[LAGS + i - lag]
                sums[level, lag - 1] = part

    def segment(phase, carry):
        seg = lax.rem(tm + pick(ORDER, phase) + N_TM, N_TM)

        @pl.when(phase == 0)
        def _():
            part = xs.at[pl.ds(LAGS, (N_PIX - 1) * READ)]
            pltpu.make_async_copy(part, part, recv_sem.at[seg]).wait()

        @pl.when(phase > 0)
        def _():
            part = xs.at[pl.ds(LAGS, N_PIX * READ)]
            pltpu.make_async_copy(part, part, recv_sem.at[seg]).wait()

        joined = (pick([before_done(i, -1) for i in range(N_TM)], phase) > 0) & (seg > 0)
        for level, (buf, deeper) in enumerate(((xs, s1), (s1, s2), (s2, s3), (s3, None))):
            level_pass(level, buf, deeper, seg, joined)
        after = lax.rem(seg + 1, N_TM)

        @pl.when((pick([before_done(i, 1) for i in range(N_TM)], phase) > 0) & (after > 0))
        def _():
            border(after)

        return carry

    lax.fori_loop(0, N_TM, segment, 0)

    total = s3[LAGS]
    for i in range(1, FRAMES >> 3):
        total = total + s3[LAGS + i]
    mean = total / (FRAMES >> 3)
    keeper = consts[2]
    scale = keeper / (mean * mean)
    shown = mean * keeper
    mean_out[...] = shown
    flat_sums = rows_tmp
    for level in range(LEVELS):
        for half in range(2):
            for k in range(8):
                lag = half * 8 + k
                flat_sums[half, pl.ds(k * 8, 8), :] = sums[level, lag] * (scale * (1.0 / ((FRAMES >> level) - lag - 1)))
            for j in range(8):
                g2_out[level, pl.ds(half * 8, 8), pl.ds(j * BLK, BLK)] = flat_sums[half, pl.ds(j, 8, stride=8), :]

    sent = xs.at[pl.ds(LAGS, (N_DEV - 1) * READ)]
    pltpu.make_async_copy(sent, sent, send_sem).wait()


def body(raw_frames, frame_order, owner_map, pixel_mask, dark, flat, polarization, solid_angle):
    n_blocks = owner_map.shape[0]
    tiles = [a.reshape(n_blocks, BLK) for a in (dark, flat, polarization, solid_angle, pixel_mask)]
    hbm = pl.BlockSpec(memory_space=pl.ANY)
    smem = pl.BlockSpec(memory_space=pltpu.SMEM)
    vmem = pl.BlockSpec(memory_space=pltpu.VMEM)
    f32 = jnp.float32
    blocks = raw_frames.reshape(READ, n_blocks, BLK).transpose(1, 0, 2)
    g2, mean = pl.pallas_call(
        kernel,
        out_shape=(
            jax.ShapeDtypeStruct((LEVELS, LAGS, 8 * BLK), f32),
            jax.ShapeDtypeStruct((8, BLK), f32),
        ),
        in_specs=[smem, smem] + [hbm] * 6,
        out_specs=(vmem, vmem),
        scratch_shapes=[
            pltpu.VMEM(blocks.shape, f32),
            pltpu.VMEM((GROUP, 8, 8, BLK), f32),
            pltpu.VMEM((N_DEV, READ, 8, BLK), f32),
            pltpu.VMEM((LAGS + FRAMES, 8, BLK), f32),
            pltpu.VMEM((LAGS + FRAMES // 2, 8, BLK), f32),
            pltpu.VMEM((LAGS + FRAMES // 4, 8, BLK), f32),
            pltpu.VMEM((LAGS + FRAMES // 8, 8, BLK), f32),
            pltpu.VMEM((LEVELS, LAGS, 8, BLK), f32),
            pltpu.VMEM((3, 8, BLK), f32),
        ]
        + [pltpu.VMEM((n_blocks, BLK), f32)] * 4
        + [
            pltpu.VMEM((n_blocks, BLK), jnp.int32),
            pltpu.SemaphoreType.DMA,
            pltpu.SemaphoreType.DMA((5,)),
            pltpu.SemaphoreType.DMA,
            pltpu.SemaphoreType.DMA,
            pltpu.SemaphoreType.DMA((N_TM,)),
        ],
        compiler_params=pltpu.CompilerParams(collective_id=0, has_side_effects=True),
    )(owner_map, frame_order, blocks, *tiles)
    return g2, mean.reshape(8 * BLK)


def solution(mesh):
    return jax.shard_map(
        body,
        mesh=mesh,
        in_specs=(P(("tm", "pix"), None), P(("tm", "pix")), P(), P(), P(), P(), P(), P()),
        out_specs=(P(None, None, ("pix", "tm")), P(("pix", "tm"))),
        check_vma=False,
    )
```

time: 94.7 us -> 72.1 us (0.76)
  Pallas kernels: 90.8 us -> 68.3 us
    pallas_call x1, Pallas kernels: 79.8 us -> 68.3 us  [body(): pl.pallas_call(kernel, out_shape=(jax.ShapeDtypeStruct((LEVELS, LAGS, 8 *...]
    pallas_call x1 -> x0, Pallas kernels: 11 us -> none  [body(): pl.pallas_call(stage_kernel, out_shape=(jax.ShapeDtypeStruct((N_DEV, READ...]
where the time goes in v2:
time: 72.1 us; the launch traced here: 71.8 us
  Pallas kernels  68.3 us (95%)
  local copies, waits for them, and re-layouts  2.95 us (4%)
    pallas_call x1, Pallas kernels, body(): pl.pallas_call(kernel, out_shape=(jax.ShapeDtypeStruct((LEVELS, LAGS, 8 *...  68.3 us
    unnamed x2, local copies, waits for them, and re-layouts  2.95 us

profile of v2, /device:TPU:1, one launch (start us, length us, event | category | flops | bytes accessed | tf_op | source)
XLA Modules:
  0.0 71.8 jit_solution(1879455477257453595)
XLA Ops:
  0.6 68.3 %shard_map.95 = (f32[4,16,1024]{2,1,0:T(8,128)}, f32[8,128]{1,0:T(8,128)}) custom-call(s32[1024]{0:T(1024)} %owner.1, s32[8]{0:T(128)} %order.1, f32[1024,8,128]{2,1,0:T(8,128)} %bitcast.9, f32[1024,128]{1,0:T(8,128)} %bitcast.10, f32[1024,128]{1,0:T(8,128)} %bitcast.11, f32[1024,128]{1,0:T(8,128)} %bitcast.12, f32[1024,128]{1,0:T(8,128)} %bitcast.13, ...), custom_call_target="tpu_custom_call" | custom-call | tf_op jit(solution)/shard_map/pallas_call | solution.py:224
  68.9 1.7 %copy.12 = f32[4,16,1024]{2,1,0:T(8,128)} copy(f32[4,16,1024]{2,1,0:T(8,128)} %get-tuple-element.8) | data formatting | bytes 524288
  70.6 1.3 %copy.13 = f32[1024]{0:T(1024)} copy(f32[1024]{0:T(1024)} %bitcast.15) | data formatting | bytes 8192

commit v3 on v2

--- a/solution.py
+++ b/solution.py
@@ -34,12 +34,12 @@
 
 
 def step_target(step, pix, tm):
+    core = lax.rem(tm, 2)
     turn = lax.rem(step, 32)
-    at = lax.div(turn, 2)
-    offset = pick(ORDER, lax.div(step, 32) * 2 + lax.rem(turn, 2))
-    x, y = lax.div(pix, SIDE), lax.rem(pix, SIDE)
-    to_x = lax.rem(x + at, SIDE)
-    to_y = lax.rem(y + at + lax.div(at, SIDE), SIDE)
+    offset = pick(ORDER, lax.div(step, 32) * 2 + lax.rem(turn + core, 2))
+    at = lax.div(turn, 2) + 8 * core
+    to_x = lax.rem(lax.div(pix, SIDE) + at, SIDE)
+    to_y = lax.rem(lax.rem(pix, SIDE) + at + lax.div(at, SIDE), SIDE)
     return to_x * SIDE + to_y, lax.rem(tm - offset + N_TM, N_TM)
 
 
@@ -52,15 +52,21 @@
     return sums
 
 
-def kernel(owner, order, raw_in, dark_in, flat_in, pol_in, solid_in, mask_in, g2_out, mean_out,
-           raw_v, tmp, stage, xs, s1, s2, s3, sums, consts, dark_v, flat_v, pol_v, solid_v, mask_v,
-           load_sem, const_sem, own_sem, send_sem, recv_sem):
+def kernel(owner_in, order_in, raw_in, dark_in, flat_in, pol_in, solid_in, mask_in, sums, ends,
+           raw_v, tmp, stage, xs, s1, s2, s3, consts, dark_v, flat_v, pol_v, solid_v, mask_v,
+           owner, order, load_sem, map_sem, const_sem, own_sem, send_sem, recv_sem):
     pix = lax.axis_index("pix")
     tm = lax.axis_index("tm")
     me = pix * N_TM + tm
 
     load = pltpu.make_async_copy(raw_in, raw_v, load_sem)
     load.start()
+    maps = [
+        pltpu.make_async_copy(owner_in, owner, map_sem.at[0]),
+        pltpu.make_async_copy(order_in, order, map_sem.at[1]),
+    ]
+    for copy in maps:
+        copy.start()
 
     barrier = pltpu.get_barrier_semaphore()
 
@@ -89,6 +95,8 @@
         for lag in range(LAGS):
             sums[level, lag] = zero
     load.wait()
+    for copy in maps:
+        copy.wait()
     rows_tmp = tmp.reshape(GROUP, 64, BLK)
 
     def put(turn, carry):
@@ -117,20 +125,25 @@
 
     def send(step, carry):
         to_pix, to_tm = step_target(step, pix, tm)
-        pltpu.make_async_remote_copy(
-            src_ref=stage.at[to_pix * N_TM + to_tm],
-            dst_ref=my_rows,
-            send_sem=send_sem,
-            recv_sem=recv_sem.at[tm],
-            device_id={"pix": to_pix, "tm": to_tm},
-            device_id_type=MESH,
-        ).start()
+        to = to_pix * N_TM + to_tm
+
+        @pl.when(to != me)
+        def _():
+            pltpu.make_async_remote_copy(
+                src_ref=stage.at[to],
+                dst_ref=my_rows,
+                send_sem=send_sem,
+                recv_sem=recv_sem.at[tm],
+                device_id={"pix": to_pix, "tm": to_tm},
+                device_id_type=MESH,
+            ).start()
+
         return carry
 
     own = pltpu.make_async_copy(stage.at[me], my_rows, own_sem)
     own.start()
     pl.semaphore_wait(barrier, N_DEV - 1)
-    lax.fori_loop(1, N_DEV, send, 0)
+    lax.fori_loop(0, N_DEV, send, 0)
     own.wait()
 
     def level_pass(level, buf, deeper, seg, joined):
@@ -195,39 +208,43 @@
     total = s3[LAGS]
     for i in range(1, FRAMES >> 3):
         total = total + s3[LAGS + i]
-    mean = total / (FRAMES >> 3)
-    keeper = consts[2]
+    ends[0] = total / (FRAMES >> 3)
+    ends[1] = consts[2]
+
+    sent = xs.at[pl.ds(LAGS, (N_DEV - 1) * READ)]
+    pltpu.make_async_copy(sent, sent, send_sem).wait()
+
+
+def finish_kernel(sums, ends, g2_out, mean_out, rows):
+    mean, keeper = ends[0], ends[1]
     scale = keeper / (mean * mean)
-    shown = mean * keeper
-    mean_out[...] = shown
-    flat_sums = rows_tmp
+    mean_out[...] = mean * keeper
     for level in range(LEVELS):
         for half in range(2):
+            slot = level * 2 + half
             for k in range(8):
                 lag = half * 8 + k
-                flat_sums[half, pl.ds(k * 8, 8), :] = sums[level, lag] * (scale * (1.0 / ((FRAMES >> level) - lag - 1)))
+                rows[slot, pl.ds(k * 8, 8), :] = sums[level, lag] * (scale * (1.0 / ((FRAMES >> level) - lag - 1)))
+    for level in range(LEVELS):
+        for half in range(2):
             for j in range(8):
-                g2_out[level, pl.ds(half * 8, 8), pl.ds(j * BLK, BLK)] = flat_sums[half, pl.ds(j, 8, stride=8), :]
-
-    sent = xs.at[pl.ds(LAGS, (N_DEV - 1) * READ)]
-    pltpu.make_async_copy(sent, sent, send_sem).wait()
+                g2_out[level, pl.ds(half * 8, 8), pl.ds(j * BLK, BLK)] = rows[level * 2 + half, pl.ds(j, 8, stride=8), :]
 
 
 def body(raw_frames, frame_order, owner_map, pixel_mask, dark, flat, polarization, solid_angle):
     n_blocks = owner_map.shape[0]
     tiles = [a.reshape(n_blocks, BLK) for a in (dark, flat, polarization, solid_angle, pixel_mask)]
     hbm = pl.BlockSpec(memory_space=pl.ANY)
-    smem = pl.BlockSpec(memory_space=pltpu.SMEM)
     vmem = pl.BlockSpec(memory_space=pltpu.VMEM)
     f32 = jnp.float32
     blocks = raw_frames.reshape(READ, n_blocks, BLK).transpose(1, 0, 2)
-    g2, mean = pl.pallas_call(
+    sums, ends = pl.pallas_call(
         kernel,
         out_shape=(
-            jax.ShapeDtypeStruct((LEVELS, LAGS, 8 * BLK), f32),
-            jax.ShapeDtypeStruct((8, BLK), f32),
+            jax.ShapeDtypeStruct((LEVELS, LAGS, 8, BLK), f32),
+            jax.ShapeDtypeStruct((2, 8, BLK), f32),
         ),
-        in_specs=[smem, smem] + [hbm] * 6,
+        in_specs=[hbm] * 8,
         out_specs=(vmem, vmem),
         scratch_shapes=[
             pltpu.VMEM(blocks.shape, f32),
@@ -237,13 +254,15 @@
             pltpu.VMEM((LAGS + FRAMES // 2, 8, BLK), f32),
             pltpu.VMEM((LAGS + FRAMES // 4, 8, BLK), f32),
             pltpu.VMEM((LAGS + FRAMES // 8, 8, BLK), f32),
-            pltpu.VMEM((LEVELS, LAGS, 8, BLK), f32),
             pltpu.VMEM((3, 8, BLK), f32),
         ]
         + [pltpu.VMEM((n_blocks, BLK), f32)] * 4
         + [
             pltpu.VMEM((n_blocks, BLK), jnp.int32),
+            pltpu.SMEM(owner_map.shape, jnp.int32),
+            pltpu.SMEM(frame_order.shape, jnp.int32),
             pltpu.SemaphoreType.DMA,
+            pltpu.SemaphoreType.DMA((2,)),
             pltpu.SemaphoreType.DMA((5,)),
             pltpu.SemaphoreType.DMA,
             pltpu.SemaphoreType.DMA,
@@ -251,6 +270,16 @@
         ],
         compiler_params=pltpu.CompilerParams(collective_id=0, has_side_effects=True),
     )(owner_map, frame_order, blocks, *tiles)
+    g2, mean = pl.pallas_call(
+        finish_kernel,
+        out_shape=(
+            jax.ShapeDtypeStruct((LEVELS, LAGS, 8 * BLK), f32),
+            jax.ShapeDtypeStruct((8, BLK), f32),
+        ),
+        in_specs=[vmem, vmem],
+        out_specs=(vmem, vmem),
+        scratch_shapes=[pltpu.VMEM((2 * LEVELS, 64, BLK), f32)],
+    )(sums, ends)
     return g2, mean.reshape(8 * BLK)
 
 

time: 72.1 us -> 68.5 us (0.950)
  local copies, waits for them, and re-layouts: 2.95 us -> 0 us
  Pallas kernels: 68.3 us -> 67 us
    unnamed x2 -> x0, local copies, waits for them, and re-layouts: 2.95 us -> none
    pallas_call x1 -> x2, Pallas kernels: 68.3 us -> 67 us  [the longest x1 65.2 us: body(): pl.pallas_call(kernel, out_shape=(jax.ShapeDtypeStruct((LEVELS, LAGS, 8,...]
where the time goes in v3:
time: 68.5 us; the launch traced here: 67.6 us
  Pallas kernels  67 us (98%)
    pallas_call x1, Pallas kernels, body(): pl.pallas_call(kernel, out_shape=(jax.ShapeDtypeStruct((LEVELS, LAGS, 8,...  65.2 us
    pallas_call x1, Pallas kernels, body(): pl.pallas_call(finish_kernel, out_shape=(jax.ShapeDtypeStruct((LEVELS, LA...  1.74 us

profile of v3, /device:TPU:1, one launch (start us, length us, event | category | flops | bytes accessed | tf_op | source)
XLA Modules:
  0.0 67.6 jit_solution(15019066951807145649)
XLA Ops:
  0.6 65.2 %shard_map.95 = (f32[4,16,8,128]{3,2,1,0:T(8,128)}, f32[2,8,128]{2,1,0:T(8,128)}) custom-call(s32[1024]{0:T(1024)} %owner_in.1, s32[8]{0:T(128)} %order_in.1, f32[1024,8,128]{2,1,0:T(8,128)} %bitcast.9, f32[1024,128]{1,0:T(8,128)} %bitcast.10, f32[1024,128]{1,0:T(8,128)} %bitcast.11, f32[1024,128]{1,0:T(8,128)} %bitcast.12, f32[1024,128]{1,0:T(8,128)} %bitcast.13, ...), custom_call_target="tpu_custom_call" | custom-call | tf_op jit(solution)/shard_map/pallas_call | solution.py:241
  65.9 1.7 %shard_map.96 = (f32[4,16,1024]{2,1,0:T(8,128)}, f32[8,128]{1,0:T(8,128)}) custom-call(f32[4,16,8,128]{3,2,1,0:T(8,128)} %get-tuple-element.6.sums, f32[2,8,128]{2,1,0:T(8,128)} %get-tuple-element.7.ends), custom_call_target="tpu_custom_call" | custom-call | tf_op jit(solution)/shard_map/pallas_call | solution.py:273
